TPU v7x, 128 devices: a whole 4x4x4 slice. The times are simulated.
128 devices in a mesh: seq: 8 (over x, core), tensor: 8 (over z, y_lo), dp: 2 (over y_hi).
Axes of the slice: x: 4, y: 4 (y_hi: 2, y_lo: 2; y = y_hi * 2 + y_lo), z: 4, core: 2. Of those that a mesh axis runs over, the one named last changes fastest.
Arguments:
- ssm_input: bfloat16 [2, 2048, 8192], P('dp', 'seq', 'tensor'), may hold values from -6 to 6
- b_input: bfloat16 [2, 2048, 1024], P('dp', 'seq', 'tensor'), may hold values from -0.125 to 0.125
- c_input: bfloat16 [2, 2048, 1024], P('dp', 'seq', 'tensor'), may hold values from -0.125 to 0.125
- step_size: float32 [2, 128, 2048], P('dp', 'tensor', 'seq'), may hold values from 0 to 2048, as said below
- decay_rate: float32 [128], P('tensor'), may hold values from 0 to 1, as said below
- skip_gain: float32 [128], P('tensor'), may hold values from 0.5 to 2
- resets: int32 [2, 8], P('dp', 'seq'), may hold values 0 or 1
- out_grad: bfloat16 [2, 2048, 4096], P('dp', 'seq'), may hold values from -6 to 6
- out_weight: bfloat16 [4096, 8192], P(('seq', 'dp'), 'tensor'), may hold values from -0.0625 to 0.0625
Outputs:
- grad_input: bfloat16 [2, 2048, 8192], P('dp', 'seq', 'tensor')
- grad_b: float32 [2, 2048, 1024], P('dp', 'seq', 'tensor')
- grad_c: float32 [2, 2048, 1024], P('dp', 'seq', 'tensor')
- grad_weight: float32 [4096, 8192], P(('seq', 'dp'), 'tensor')
Inputs may be any that keep to these rules, and one draw needn't show every extreme that they name: `step_size`: positive per-position steps. `decay_rate`: positive per-head rates.
All inputs are finite; a program needn't handle non-finite values. No bound on the sum of `resets` on one device may be relied on, other than what follows from the above.
Results may differ from a plain program's by a relative error of at most 0.017.
Values may be sent and summed in bfloat16 or wider, within the bound.
A program may use at most 128 MiB of HBM per device.

v0:
```python
import jax
import jax.numpy as jnp
from jax import lax
from jax.sharding import PartitionSpec as P

P_SIZE = 64
N = 128
Q = 256


def prefix(value, axis, join, neutral, backward):
    count, mine = (lax.axis_size(axis), lax.axis_index(axis))
    pieces = jax.tree.map(lambda part: lax.all_gather(part, axis), value)
    if backward:
        pieces = jax.tree.map(lambda part: part[::-1], pieces)
        mine = count - 1 - mine
    running = jax.tree.map(
        lambda part, zero: jnp.full_like(part, 0) + jnp.asarray(zero, part.dtype), value, neutral
    )

    def step(position, running):
        longer = join(running, jax.tree.map(lambda part: part[position], pieces))
        return jax.tree.map(lambda new, old: jnp.where(position < mine, new, old), longer, running)

    return lax.fori_loop(0, count - 1, step, running)


def contract(pattern, former, latter):
    return jnp.einsum(pattern, former, latter, preferred_element_type=jnp.float32)


def block_tables(step_rows, head_rates):
    log_decay = jnp.cumsum(-step_rows * head_rates[..., None], axis=-1)
    last_log = log_decay[..., -1:]
    damping = jnp.exp(last_log[..., 0])
    to_end = jnp.moveaxis(jnp.exp(last_log - log_decay), -1, 0)[..., None]
    from_start = jnp.moveaxis(jnp.exp(log_decay), -1, 0)[..., None]
    positions = jnp.arange(log_decay.shape[-1])
    causal = positions[:, None] >= positions[None, :]
    spread = log_decay[..., :, None] - log_decay[..., None, :]
    weights = jnp.where(causal, jnp.exp(jnp.minimum(spread, 0.0)), 0.0)
    return (damping, to_end, from_start, weights)


def block_sums(inputs, b_rows, c_rows, grad_rows, to_end, from_start):
    weighted_in = (inputs.astype(jnp.float32) * to_end).astype(jnp.bfloat16)
    weighted_grad = (grad_rows.astype(jnp.float32) * from_start).astype(jnp.bfloat16)
    carried = contract("qgkp,qgn->gkpn", weighted_in, b_rows)
    adjoint = contract("qgkp,qgn->gkpn", weighted_grad, c_rows)
    return (carried, adjoint, weighted_in, weighted_grad)


def block_grads(
    inputs,
    b_rows,
    c_rows,
    grad_rows,
    skip_rows,
    to_end,
    from_start,
    weights,
    weighted_in,
    weighted_grad,
    state_in,
    adjoint_out,
):
    scores = contract("ign,jgn->gij", c_rows, b_rows)
    mixing = (weights * scores[:, None]).astype(jnp.bfloat16)
    skip_term = skip_rows[None, :, :, None]
    output = (
        contract("gkij,jgkp->igkp", mixing, inputs)
        + from_start * contract("gkpn,ign->igkp", state_in, c_rows)
        + skip_term * inputs.astype(jnp.float32)
    )
    grad_in = (
        contract("gkij,igkp->jgkp", mixing, grad_rows)
        + to_end * contract("gkpn,jgn->jgkp", adjoint_out, b_rows)
        + skip_term * grad_rows.astype(jnp.float32)
    )
    products = contract("igkp,jgkp->gkij", grad_rows, inputs)
    paired = (weights * products).astype(jnp.bfloat16)
    grad_b = contract("gkij,ign->jgn", paired, c_rows) + contract(
        "jgkp,gkpn->jgn", weighted_in, adjoint_out
    )
    grad_c = contract("gkij,jgn->ign", paired, b_rows) + contract(
        "igkp,gkpn->ign", weighted_grad, state_in
    )
    return (output.astype(jnp.bfloat16), grad_in.astype(jnp.bfloat16), grad_b, grad_c)


def forward_step(running, sliced):
    kept, carried, damping = sliced
    state_in = kept * running
    return (damping[..., None, None] * state_in + carried, state_in)


def backward_step(running, sliced):
    kept, adjoint, damping = sliced
    return (kept * (damping[..., None, None] * running + adjoint), running)


def compose(earlier, following):
    return (earlier[0] * following[0], following[0][..., None, None] * earlier[1] + following[1])


def body(
    ssm_input, b_input, c_input, step_size, decay_rate, skip_gain, resets, out_grad, out_weight
):
    head_count = decay_rate.shape[0]
    length = ssm_input.shape[1]
    blocks = length // Q
    incoming = out_grad[0]
    columns = incoming
    head_total = jnp.dot(
        columns,
        lax.all_gather(out_weight, ("seq", "dp"), axis=0, tiled=True),
        preferred_element_type=jnp.float32,
    )
    head_grad = head_total.astype(jnp.bfloat16)
    inputs = ssm_input[0].reshape(blocks, Q, 1, head_count, P_SIZE)
    b_rows = b_input[0].reshape(blocks, Q, 1, N)
    c_rows = c_input[0].reshape(blocks, Q, 1, N)
    grad_rows = head_grad.reshape(blocks, Q, 1, head_count, P_SIZE)
    step_rows = step_size[0].reshape(1, head_count, blocks, Q).transpose(2, 0, 1, 3)
    head_rates = decay_rate.reshape(1, head_count)
    skip_rows = skip_gain.reshape(1, head_count)
    keep_rows = (1 - resets[0]).astype(jnp.float32)
    decays, to_end, from_start, weights = jax.vmap(block_tables, in_axes=(0, None))(
        step_rows, head_rates
    )
    carried, adjoint, weighted_in, weighted_grad = jax.vmap(block_sums)(
        inputs, b_rows, c_rows, grad_rows, to_end, from_start
    )
    zero_state = jnp.zeros((1, head_count, P_SIZE, N), jnp.float32)
    local_out, local_states = lax.scan(forward_step, zero_state, (keep_rows, carried, decays))
    local_back, local_adjoints = lax.scan(
        backward_step, zero_state, (keep_rows, adjoint, decays), reverse=True
    )
    factors = keep_rows[:, None, None] * decays
    through = jnp.prod(factors, axis=0)
    unit_gain = jnp.ones_like(through)
    through_before, state_before = prefix(
        (through, local_out), "seq", compose, (unit_gain, zero_state), False
    )
    through_after, adjoint_after = prefix(
        (through, local_back), "seq", compose, (unit_gain, zero_state), True
    )
    final_state, states = lax.scan(forward_step, state_before, (keep_rows, carried, decays))
    final_adjoint, adjoints = lax.scan(
        backward_step, adjoint_after, (keep_rows, adjoint, decays), reverse=True
    )
    output, grad_in, grad_b, grad_c = jax.vmap(
        block_grads, in_axes=(0, 0, 0, 0, None, 0, 0, 0, 0, 0, 0, 0)
    )(
        inputs,
        b_rows,
        c_rows,
        grad_rows,
        skip_rows,
        to_end,
        from_start,
        weights,
        weighted_in,
        weighted_grad,
        states.astype(jnp.bfloat16),
        adjoints.astype(jnp.bfloat16),
    )
    outputs = output.reshape(length, head_count * P_SIZE)
    columns = incoming
    grad_weight = lax.psum_scatter(
        jnp.einsum("ld,lh->dh", columns, outputs, preferred_element_type=jnp.float32).astype(
            jnp.bfloat16
        ),
        ("seq", "dp"),
        scatter_dimension=0,
        tiled=True,
    ).astype(jnp.float32)
    return (
        grad_in.reshape(1, length, head_count * P_SIZE),
        grad_b.reshape(1, length, N),
        grad_c.reshape(1, length, N),
        grad_weight,
    )


def solution(mesh):
    in_specs = (
        P("dp", "seq", "tensor"),
        P("dp", "seq", "tensor"),
        P("dp", "seq", "tensor"),
        P("dp", "tensor", "seq"),
        P("tensor"),
        P("tensor"),
        P("dp", "seq"),
        P("dp", "seq", None),
        P(("seq", "dp"), "tensor"),
    )
    out_specs = (
        P("dp", "seq", "tensor"),
        P("dp", "seq", "tensor"),
        P("dp", "seq", "tensor"),
        P(("seq", "dp"), "tensor"),
    )
    return jax.shard_map(body, mesh=mesh, in_specs=in_specs, out_specs=out_specs, check_vma=False)
```

profile of v0, /device:TPU:1, one launch (start us, length us, event | category | flops | bytes accessed | tf_op | source)
XLA Modules:
  0.0 289.9 jit_solution(8070474870886657349)
XLA Ops:
  11.7 1.3 copy.106
  13.9 1.9 convolution_add_fusion
  18.0 12.0 %all-gather = f32[8,1,16,1]{2,3,1,0:T(1,128)S(1)} all-gather(f32[1,1,16,1]{2,3,1,0:T(1,128)} %get-tuple-element.390), channel_id=2, replica_groups=mesh['seq'=8,'tensor'=8,'dp'=2] {'seq'}, dimensions={0}, use_global_device_ids=true | all-gather | bytes 576 | tf_op jit(solution)/shard_map/all_gather | solution.py:13
  31.7 20.0 %all-gather.11.cloned.1.call-done = f32[128,64,128]{2,1,0:T(8,128)} async-done(((f32[16,64,128]{2,1,0:T(8,128)}), f32[128,64,128]{2,1,0:T(8,128)}) %all-gather.11.cloned.1.call-update) | async-done | bytes 4194320 | tf_op jit(solution)/shard_map/all_gather | solution.py:13
  51.7 8.5 %while.19 = (s32[]{:T(128)}, f32[1,16,64,128]{3,2,1,0:T(8,128)S(1)}, s32[]{:T(128)}, f32[8,1,16]{2,1,0:T(1,128)S(1)}, f32[8,1,16,64,128]{4,3,2,1,0:T(8,128)}, /*index=5*/s32[]{:T(128)}, s32[]{:T(128)}) while((s32[]{:T(128)}, f32[1,16,64,128]{3,2,1,0:T(8,128)S(1)}, s32[]{:T(128)}, f32[8,1,16]{2,1,0:T(1,128)S(1)}, ...), condition=%wide.region_6.7_spmd.clone, body=%wide.region_5.6_spmd.clone.sunk | while | flops 524292 | bytes 1573161 | solution.py:25
  51.7 1.2 fusion.61
  52.9 1.2 fusion.61
  60.5 2.5 fusion.21
  63.0 5.7 %convert_bitcast_fusion = bf16[4096,1024]{0,1:T(8,128)(2,1)} fusion(bf16[256,1024]{0,1:T(8,128)(2,1)S(1)} %bitcast.203, bf16[1,256,4096]{2,1,0:T(8,128)(2,1)S(1)} %copy-done), kind=kOutput, calls=%fused_computation.6 | convolution fusion | flops 2151677952 | bytes 11010048 | tf_op jit(solution)/shard_map/ld,lh->dh/dot_general | solution.py:171
  70.0 2.6 copy.101
  72.6 54.2 %all-gather.7.cloned.1.call-done = bf16[4096,1024]{1,0:T(8,128)(2,1)} async-done(((bf16[256,1024]{1,0:T(8,128)(2,1)}), bf16[4096,1024]{1,0:T(8,128)(2,1)}) %all-gather.7.cloned.1.call-update) | async-done | bytes 8388624 | tf_op jit(solution)/shard_map/all_gather | solution.py:116
  126.8 7.0 %multiply_convert_fusion.20 = (bf16[256,1024]{1,0:T(8,128)(2,1)}, bf16[256,1024]{1,0:T(8,128)(2,1)}) fusion(f32[256,1024]{1,0:T(8,128)} %copy.101, bf16[4096,1024]{1,0:T(8,128)(2,1)} %all-gather.7.cloned.1.call-done, bf16[1,256,4096]{2,1,0:T(8,128)(2,1)S(1)} %copy-done), kind=kOutput, calls=%fused_computation.44 | convolution fusion | flops 2148532224 | bytes 12582912 | tf_op jit(solution)/shard_map/dot_general | solution.py:114
  133.8 1.2 copy.102
  136.3 2.2 copy.93
  138.5 2.3 copy.105
  140.7 1.5 convolution_bitcast_fusion.2
  142.2 2.8 convert_reduce_fusion
  145.8 84.1 %reduce-scatter.2.cloned.1.call-done = bf16[256,1024]{0,1:T(8,128)(2,1)} async-done(((bf16[4096,1024]{0,1:T(8,128)(2,1)}), bf16[256,1024]{0,1:T(8,128)(2,1)}) %reduce-scatter.2.cloned.1.call-update) | async-done | bytes 524304 | tf_op jit(solution)/shard_map/reduce_scatter | solution.py:170
  230.0 2.2 copy.113
  232.2 32.5 %all-gather.9.cloned.1.call-done = f32[128,64,128]{2,1,0:T(8,128)} async-done(((f32[16,64,128]{2,1,0:T(8,128)}), f32[128,64,128]{2,1,0:T(8,128)}) %all-gather.9.cloned.1.call-update) | async-done | bytes 4194320 | tf_op jit(solution)/shard_map/all_gather | solution.py:13
  264.6 4.9 %rev.7 = f32[8,1,16,64,128]{4,3,2,1,0:T(8,128)} reverse(f32[8,1,16,64,128]{4,3,2,1,0:T(8,128)} %bitcast.191), dimensions={0} | reverse | bytes 8388608 | tf_op jit(solution)/shard_map/rev | solution.py:15
  269.5 8.5 %while.18 = (s32[]{:T(128)}, f32[1,16,64,128]{3,2,1,0:T(8,128)S(1)}, s32[]{:T(128)}, f32[8,1,16]{2,1,0:T(1,128)S(1)}, f32[8,1,16,64,128]{4,3,2,1,0:T(8,128)}, /*index=5*/s32[]{:T(128)}, s32[]{:T(128)}) while((s32[]{:T(128)}, f32[1,16,64,128]{3,2,1,0:T(8,128)S(1)}, s32[]{:T(128)}, f32[8,1,16]{2,1,0:T(1,128)S(1)}, ...), condition=%wide.region_3.4_spmd.clone, body=%wide.region_2.3_spmd.clone.sunk | while | flops 524292 | bytes 1573161 | solution.py:25
  269.5 1.2 fusion.60
  278.7 2.8 fusion.20
  (90 shorter events, 27.6 us)
Async XLA Ops:
  7.2 55.8 %copy-start = (bf16[1,256,4096]{2,1,0:T(8,128)(2,1)S(1)}, bf16[1,256,4096]{2,1,0:T(8,128)(2,1)}, u32[]{:S(2)}) copy-start(bf16[1,256,4096]{2,1,0:T(8,128)(2,1)} %param.20) | copy-start | bytes 6291460
  7.2 23.6 %copy-start.5 = (bf16[1,256,128]{2,1,0:T(8,128)(2,1)S(1)}, bf16[1,256,128]{2,1,0:T(8,128)(2,1)}, u32[]{:S(2)}) copy-start(bf16[1,256,128]{2,1,0:T(8,128)(2,1)} %param.14) | copy-start | bytes 196612
  7.2 23.6 %copy-start.6 = (bf16[1,256,128]{2,1,0:T(8,128)(2,1)S(1)}, bf16[1,256,128]{2,1,0:T(8,128)(2,1)}, u32[]{:S(2)}) copy-start(bf16[1,256,128]{2,1,0:T(8,128)(2,1)} %param.15) | copy-start | bytes 196612
  7.2 44.5 %all-gather.11.cloned.1.call-start = ((), (), s32[]{:S(2)}) async-start(), calls=%async_computation.4 | async-start | bytes 4718592 | tf_op jit(solution)/shard_map/all_gather | solution.py:13
  12.9 47.6 %copy-start.4 = (bf16[1,256,1024]{1,2,0:T(8,128)(2,1)}, bf16[1,256,1024]{1,2,0:T(8,128)(2,1)S(1)}, u32[]{:S(2)}) copy-start(bf16[1,256,1024]{1,2,0:T(8,128)(2,1)S(1)} %copy.106) | copy-start | bytes 1572868
  13.0 0.8 copy-start.2
  15.8 111.0 %all-gather.7.cloned.1.call-start = ((), (), s32[]{:S(2)}) async-start(), calls=%async_computation.1 | async-start | bytes 8912896 | tf_op jit(solution)/shard_map/all_gather | solution.py:116
  16.6 213.4 %reduce-scatter.2.cloned.1.call-start = ((), (), s32[]{:S(2)}) async-start(), calls=%async_computation.2 | async-start | bytes 8912896 | tf_op jit(solution)/shard_map/reduce_scatter | solution.py:170
  30.0 112.2 %copy-start.8 = (pred[256,256]{1,0:T(8,128)(4,1)}, pred[256,256]{1,0:T(8,128)(4,1)S(1)}, u32[]{:S(2)}) copy-start(pred[256,256]{1,0:T(8,128)(4,1)S(1)} %iota_compare_fusion) | copy-start | bytes 196612
  30.8 111.4 %copy-start.9 = (f32[16,256]{1,0:T(8,128)}, f32[16,256]{1,0:T(8,128)S(1)}, u32[]{:S(2)}) copy-start(f32[16,256]{1,0:T(8,128)S(1)} %bitcast_add_fusion.2) | copy-start | bytes 49156
  30.8 29.4 %copy-start.7 = (f32[256,16]{0,1:T(8,128)S(1)}, f32[256,16]{0,1:T(8,128)}, u32[]{:S(2)}) copy-start(f32[256,16]{0,1:T(8,128)} %copy.100) | copy-start | bytes 49156
  51.7 8.8 %copy-start.11 = (f32[16]{0:T(128)S(1)}, f32[16]{0:T(128)}, u32[]{:S(2)}) copy-start(f32[16]{0:T(128)} %param.18) | copy-start | bytes 196
  68.7 195.9 %all-gather.9.cloned.1.call-start = ((), (), s32[]{:S(2)}) async-start(), calls=%async_computation.3 | async-start | bytes 4718592 | tf_op jit(solution)/shard_map/all_gather | solution.py:13
  72.6 62.5 %copy-start.10 = (f32[16]{0:T(128)S(1)}, f32[16]{0:T(128)}, u32[]{:S(2)}) copy-start(f32[16]{0:T(128)} %get-tuple-element.389) | copy-start | bytes 196
  135.1 1.1 copy-start.1
  269.5 8.8 %copy-start.3 = (bf16[1,256,1024]{1,2,0:T(8,128)(2,1)S(1)}, bf16[1,256,1024]{1,2,0:T(8,128)(2,1)}, u32[]{:S(2)}) copy-start(bf16[1,256,1024]{1,2,0:T(8,128)(2,1)} %copy-done.2) | copy-start | bytes 1572868
Sparse Core Ops, SparseCore 0:
  15.9 35.6 all-gather.10
  54.1 72.6 all-gather.6
  131.2 98.7 reduce-scatter.1
  232.1 32.4 all-gather.8
where the time goes:
time: 291 us; the launch traced here: 290 us
  waiting for transfers between devices  192 us (66%)
  matrix products  28.8 us (10%)
  local copies, waits for them, and re-layouts  21.4 us (7%)
  other arithmetic  20.7 us (7%)
  between operations  14.7 us (5%)
  blocking collectives  12 us (4%)
    reduce_scatter x1, waiting for transfers between devices, body(): lax.psum_scatter(jnp.einsum('ld,lh->dh', columns, outputs, preferred_elem...  84.1 us
    all_gather x1, waiting for transfers between devices, body(): lax.all_gather(out_weight, ('seq', 'dp'), axis=0, tiled=True)  54.2 us
    all_gather x2, waiting for transfers between devices, prefix(): pieces = jax.tree.map(lambda part: lax.all_gather(part, axis), value)  52.5 us
    select_n x14, other arithmetic, step(): jnp.where(position < mine, new, old)  16.5 us
    dot_general x12, matrix products, contract(): jnp.einsum(pattern, former, latter, preferred_element_type=jnp.float32)  16.1 us
    all_gather x1, blocking collectives, prefix(): pieces = jax.tree.map(lambda part: lax.all_gather(part, axis), value)  12 us
    dot_general x1, matrix products, body(): jnp.dot(columns, lax.all_gather(out_weight, ('seq', 'dp'), axis=0, tiled=...  7.02 us
  transfers between devices with their start and end apart: 4, of which 4 were waited for; matrix products, arithmetic and copies ran while one was open for 15% of the time, Pallas kernels for 0%

commit v1 on v0

--- a/solution.py
+++ b/solution.py
@@ -113,7 +113,12 @@
     columns = incoming
     head_total = jnp.dot(
         columns,
-        lax.all_gather(out_weight, ("seq", "dp"), axis=0, tiled=True),
+        jnp.concatenate(
+            lax.all_to_all(
+                jnp.stack([out_weight] * lax.axis_size(("seq", "dp"))), ("seq", "dp"), 0, 0
+            ),
+            axis=0,
+        ),
         preferred_element_type=jnp.float32,
     )
     head_grad = head_total.astype(jnp.bfloat16)

time: 291 us -> 331 us (1.14)
  waiting for transfers between devices: 192 us -> 219 us
  starting transfers between devices: 0.34 us -> 8.7 us
  blocking collectives: 12 us -> 17.3 us
    all_to_all x0 -> x1, waiting for transfers between devices: none -> 136 us  [body(): lax.all_to_all(jnp.stack([out_weight] * lax.axis_size(('seq', 'dp'))), ('...]
    all_gather x1 -> x0, waiting for transfers between devices: 54.2 us -> none  [body(): lax.all_gather(out_weight, ('seq', 'dp'), axis=0, tiled=True)]
    all_gather x2, waiting for transfers between devices: 52.5 us -> 0.01 us  [prefix(): pieces = jax.tree.map(lambda part: lax.all_gather(part, axis), value)]
    all_to_all x0 -> x1, starting transfers between devices: none -> 8.58 us  [body(): lax.all_to_all(jnp.stack([out_weight] * lax.axis_size(('seq', 'dp'))), ('...]
    all_gather x1, blocking collectives: 12 us -> 17.3 us  [prefix(): pieces = jax.tree.map(lambda part: lax.all_gather(part, axis), value)]
    another operation x6 -> x7, local copies, waits for them, and re-layouts: 0.8 us -> 5.69 us  [the longest x1 5.5 us: body(): jnp.stack([out_weight] * lax.axis_size(('seq', 'dp')))]
  transfers between devices with their start and end apart: 4 -> 4, of which waited for: 4 -> 2; matrix products, arithmetic and copies ran while one was open for 15% -> 18% of each run, Pallas kernels for 0% -> 0%
where the time goes in v1:
time: 331 us; the launch traced here: 329 us
  waiting for transfers between devices  219 us (66%)
  matrix products  28.5 us (9%)
  local copies, waits for them, and re-layouts  23.1 us (7%)
  other arithmetic  17.5 us (5%)
  blocking collectives  17.3 us (5%)
  between operations  14.7 us (4%)
  starting transfers between devices  8.7 us (3%)
    all_to_all x1, waiting for transfers between devices, body(): lax.all_to_all(jnp.stack([out_weight] * lax.axis_size(('seq', 'dp'))), ('...  136 us
    reduce_scatter x1, waiting for transfers between devices, body(): lax.psum_scatter(jnp.einsum('ld,lh->dh', columns, outputs, preferred_elem...  82.3 us
    all_gather x1, blocking collectives, prefix(): pieces = jax.tree.map(lambda part: lax.all_gather(part, axis), value)  17.3 us
    select_n x14, other arithmetic, step(): jnp.where(position < mine, new, old)  16.6 us
    dot_general x12, matrix products, contract(): jnp.einsum(pattern, former, latter, preferred_element_type=jnp.float32)  16.1 us
    all_to_all x1, starting transfers between devices, body(): lax.all_to_all(jnp.stack([out_weight] * lax.axis_size(('seq', 'dp'))), ('...  8.58 us
    dot_general x1, matrix products, body(): jnp.dot(columns, jnp.concatenate(lax.all_to_all(jnp.stack([out_weight] *...  6.8 us
  transfers between devices with their start and end apart: 4, of which 2 were waited for; matrix products, arithmetic and copies ran while one was open for 18% of the time, Pallas kernels for 0%

profile of v1, /device:TPU:1, one launch (start us, length us, event | category | flops | bytes accessed | tf_op | source)
XLA Modules:
  0.0 328.8 jit_solution(1407228045901389352)
XLA Ops:
  7.2 5.5 %stack.2 = bf16[16,256,1024]{2,1,0:T(8,128)(2,1)} broadcast(bf16[256,1024]{1,0:T(8,128)(2,1)} %param.21), dimensions={1,2} | broadcast | bytes 8912896 | tf_op jit(solution)/shard_map/stack | solution.py:118
  12.7 8.6 %all-to-all-start = ((bf16[16,256,1024]{2,1,0:T(8,128)(2,1)}), bf16[16,256,1024]{2,1,0:T(8,128)(2,1)}, u32[]{:S(2)}, u32[]{:S(2)}) async-start(bf16[16,256,1024]{2,1,0:T(8,128)(2,1)} %stack.2), calls=%async_computation | async-start | bytes 16777216 | tf_op jit(solution)/shard_map/all_to_all | solution.py:117
  23.2 1.3 copy.106
  26.7 1.3 copy.101
  28.0 136.3 %all-to-all-done = bf16[16,256,1024]{2,1,0:T(8,128)(2,1)} async-done(((bf16[16,256,1024]{2,1,0:T(8,128)(2,1)}), bf16[16,256,1024]{2,1,0:T(8,128)(2,1)}, u32[]{:S(2)}, u32[]{:S(2)}) %all-to-all-start) | async-done | bytes 8388640 | tf_op jit(solution)/shard_map/all_to_all | solution.py:117
  164.3 6.8 %multiply_convert_fusion.20 = (bf16[256,1024]{1,0:T(8,128)(2,1)S(1)}, bf16[256,1024]{1,0:T(8,128)(2,1)}) fusion(f32[256,1024]{1,0:T(8,128)} %copy.101, bf16[4096,1024]{1,0:T(8,128)(2,1)} %bitcast.1, bf16[1,256,4096]{2,1,0:T(8,128)(2,1)S(1)} %copy-done), kind=kOutput, calls=%fused_computation.44 | convolution fusion | flops 2148532224 | bytes 12582912 | tf_op jit(solution)/shard_map/dot_general | solution.py:114
  172.6 17.3 %all-gather = f32[8,1,16,1]{2,3,1,0:T(1,128)S(1)} all-gather(f32[1,1,16,1]{2,3,1,0:T(1,128)S(1)} %get-tuple-element.390), channel_id=2, replica_groups=mesh['seq'=8,'tensor'=8,'dp'=2] {'seq'}, dimensions={0}, use_global_device_ids=true | all-gather | bytes 576 | tf_op jit(solution)/shard_map/all_gather | solution.py:13
  190.9 8.6 %while.19 = (s32[]{:T(128)}, f32[1,16,64,128]{3,2,1,0:T(8,128)S(1)}, s32[]{:T(128)}, f32[8,1,16]{2,1,0:T(1,128)S(1)}, f32[8,1,16,64,128]{4,3,2,1,0:T(8,128)}, /*index=5*/s32[]{:T(128)}, s32[]{:T(128)}) while((s32[]{:T(128)}, f32[1,16,64,128]{3,2,1,0:T(8,128)S(1)}, s32[]{:T(128)}, f32[8,1,16]{2,1,0:T(1,128)S(1)}, ...), condition=%wide.region_6.7_spmd.clone, body=%wide.region_5.6_spmd.clone.sunk | while | flops 524292 | bytes 1573161 | solution.py:25
  190.9 1.3 fusion.61
  192.2 1.2 fusion.61
  199.8 2.5 fusion.21
  202.3 5.6 %convert_bitcast_fusion = bf16[4096,1024]{0,1:T(8,128)(2,1)} fusion(bf16[256,1024]{0,1:T(8,128)(2,1)S(1)} %bitcast.204, bf16[1,256,4096]{2,1,0:T(8,128)(2,1)S(1)} %copy-done), kind=kOutput, calls=%fused_computation.6 | convolution fusion | flops 2151677952 | bytes 11010048 | tf_op jit(solution)/shard_map/ld,lh->dh/dot_general | solution.py:176
  208.0 2.1 copy.93
  210.0 2.2 copy.105
  212.2 1.4 convolution_bitcast_fusion.2
  213.6 2.7 convert_reduce_fusion
  217.1 4.7 %rev.7 = f32[8,1,16,64,128]{4,3,2,1,0:T(8,128)} reverse(f32[8,1,16,64,128]{4,3,2,1,0:T(8,128)} %bitcast.192), dimensions={0} | reverse | bytes 8388608 | tf_op jit(solution)/shard_map/rev | solution.py:15
  221.8 8.5 %while.18 = (s32[]{:T(128)}, f32[1,16,64,128]{3,2,1,0:T(8,128)S(1)}, s32[]{:T(128)}, f32[8,1,16]{2,1,0:T(1,128)S(1)}, f32[8,1,16,64,128]{4,3,2,1,0:T(8,128)}, /*index=5*/s32[]{:T(128)}, s32[]{:T(128)}) while((s32[]{:T(128)}, f32[1,16,64,128]{3,2,1,0:T(8,128)S(1)}, s32[]{:T(128)}, f32[8,1,16]{2,1,0:T(1,128)S(1)}, ...), condition=%wide.region_3.4_spmd.clone, body=%wide.region_2.3_spmd.clone.sunk | while | flops 524292 | bytes 1573161 | solution.py:25
  226.7 1.2 fusion.60
  229.1 1.2 fusion.60
  230.7 3.8 %fusion.20 = bf16[1,256,1,16,64]{1,4,3,2,0:T(8,128)(2,1)} fusion(f32[1,256,1,16,64]{1,4,3,2,0:T(8,128)S(1)} %fusion.10, bf16[256,16,64]{0,2,1:T(8,128)(2,1)} %bitcast.202, f32[256,256]{1,0:T(8,128)} %fusion.40, f32[16,256]{1,0:T(8,128)S(1)} %bitcast_add_fusion.2, pred[256,256]{1,0:T(8,128)(4,1)S(1)} %iota_compare_fusion, ...), kind=kOutput, calls=%fused_computation.29 | convolution fusion | flops 140509184 | bytes 3489856 | tf_op jit(solution)/shard_map/vmap(gkij,igkp->jgkp)/dot_general | solution.py:29
  234.4 2.1 copy.112
  237.7 82.3 %reduce-scatter.2.cloned.1.call-done = bf16[256,1024]{0,1:T(8,128)(2,1)} async-done(((bf16[4096,1024]{0,1:T(8,128)(2,1)}), bf16[256,1024]{0,1:T(8,128)(2,1)}) %reduce-scatter.2.cloned.1.call-update) | async-done | bytes 524304 | tf_op jit(solution)/shard_map/reduce_scatter | solution.py:175
  320.1 2.2 copy.113
  (88 shorter events, 20.3 us)
Async XLA Ops:
  7.2 157.1 %copy-start = (bf16[1,256,4096]{2,1,0:T(8,128)(2,1)S(1)}, bf16[1,256,4096]{2,1,0:T(8,128)(2,1)}, u32[]{:S(2)}) copy-start(bf16[1,256,4096]{2,1,0:T(8,128)(2,1)} %param.20) | copy-start | bytes 6291460
  12.7 8.6 %copy-start.8 = (f32[1,16,256]{2,1,0:T(8,128)S(1)}, f32[1,16,256]{2,1,0:T(8,128)}, u32[]{:S(2)}) copy-start(f32[1,16,256]{2,1,0:T(8,128)} %param.16) | copy-start | bytes 49156
  12.7 8.7 %copy-start.9 = (f32[16]{0:T(128)S(1)}, f32[16]{0:T(128)}, u32[]{:S(2)}) copy-start(f32[16]{0:T(128)} %param.17) | copy-start | bytes 196
  12.7 12.7 %copy-start.6 = (bf16[1,256,128]{2,1,0:T(8,128)(2,1)S(1)}, bf16[1,256,128]{2,1,0:T(8,128)(2,1)}, u32[]{:S(2)}) copy-start(bf16[1,256,128]{2,1,0:T(8,128)(2,1)} %param.14) | copy-start | bytes 196612
  12.7 151.6 %all-to-all-start = ((bf16[16,256,1024]{2,1,0:T(8,128)(2,1)}), bf16[16,256,1024]{2,1,0:T(8,128)(2,1)}, u32[]{:S(2)}, u32[]{:S(2)}) async-start(bf16[16,256,1024]{2,1,0:T(8,128)(2,1)} %stack.2), calls=%async_computation | async-start | bytes 16777216 | tf_op jit(solution)/shard_map/all_to_all | solution.py:117
  21.3 169.6 %all-gather.8.cloned.1.call-start = ((), (), s32[]{:S(2)}) async-start(), calls=%async_computation.4 | async-start | bytes 4718592 | tf_op jit(solution)/shard_map/all_gather | solution.py:13
  24.4 2.1 copy-start.4
  24.5 0.8 copy-start.2
  26.5 190.6 %all-gather.6.cloned.1.call-start = ((), (), s32[]{:S(2)}) async-start(), calls=%async_computation.3 | async-start | bytes 4718592 | tf_op jit(solution)/shard_map/all_gather | solution.py:13
  164.3 7.0 %copy-start.7 = (bf16[1,256,128]{2,1,0:T(8,128)(2,1)S(1)}, bf16[1,256,128]{2,1,0:T(8,128)(2,1)}, u32[]{:S(2)}) copy-start(bf16[1,256,128]{2,1,0:T(8,128)(2,1)} %param.15) | copy-start | bytes 196612
  171.3 1.2 copy-start.1
  172.5 147.6 %reduce-scatter.2.cloned.1.call-start = ((), (), s32[]{:S(2)}) async-start(), calls=%async_computation.2 | async-start | bytes 8912896 | tf_op jit(solution)/shard_map/reduce_scatter | solution.py:175
  190.9 8.9 %copy-start.5 = (bf16[1,256,1024]{1,2,0:T(8,128)(2,1)S(1)}, bf16[1,256,1024]{1,2,0:T(8,128)(2,1)}, u32[]{:S(2)}) copy-start(bf16[1,256,1024]{1,2,0:T(8,128)(2,1)} %copy-done.4) | copy-start | bytes 1572868
  190.9 8.9 %copy-start.10 = (f32[16]{0:T(128)S(1)}, f32[16]{0:T(128)}, u32[]{:S(2)}) copy-start(f32[16]{0:T(128)} %param.18) | copy-start | bytes 196
  230.6 5.9 %copy-start.3 = (bf16[1,256,1024]{1,2,0:T(8,128)(2,1)S(1)}, bf16[1,256,1024]{1,2,0:T(8,128)(2,1)}, u32[]{:S(2)}) copy-start(bf16[1,256,1024]{1,2,0:T(8,128)(2,1)} %copy-done.2) | copy-start | bytes 1572868
Sparse Core Ops, SparseCore 0:
  26.6 95.6 all-gather.7
  172.6 42.2 all-gather.5
  219.2 100.8 reduce-scatter.1
